TPU v7x, 32 devices: a whole 2x2x4 slice. The times are simulated.
32 devices in a mesh: gx: 4 (over z), gy: 8 (over y, x, core).
Axes of the slice: x: 2, y: 2, z: 4, core: 2. Of those that a mesh axis runs over, the one named last changes fastest.
Arguments:
- features: bfloat16 [32768, 256], P(('gx', 'gy')), may hold values from -6 to 6
- self_weight_one: bfloat16 [256, 256], replicated, may hold values from -0.375 to 0.375
- neigh_weight_one: bfloat16 [256, 256], replicated, may hold values from -1.5 to 1.5
- self_weight_two: bfloat16 [256, 256], replicated, may hold values from -0.375 to 0.375
- neigh_weight_two: bfloat16 [256, 256], replicated, may hold values from -1.5 to 1.5
- degree: int32 [32768], P(('gx', 'gy')), may hold values from 128 to 383
- local_tiles: bfloat16 [1024, 128, 128], P(('gx', 'gy')), may hold values from 0 to 1, as said below
- local_coord: int32 [1024, 2], P(('gx', 'gy')), may hold values from 0 to 7, as said below
- local_count: int32 [32], P(('gx', 'gy')), may hold values from 1 to 32, as said below
- send_block: int32 [256], P(('gx', 'gy')), may hold values from 0 to 7
- boundary_tiles: bfloat16 [256, 128, 128], P(('gx', 'gy')), may hold values from 0 to 1, as said below
- boundary_row: int32 [256], P(('gx', 'gy')), may hold values from 0 to 7
- hub_rows: int32 [256], P(('gx', 'gy')), may hold values from 0 to 1023
- hub_tiles: bfloat16 [256, 128, 128], P(('gx', 'gy')), may hold values from 0 to 1, as said below
- hub_coord: int32 [256, 2], P(('gx', 'gy')), may hold values from 0 to 7, as said below
Outputs:
- node_out: bfloat16 [32768, 256], P(('gx', 'gy'))
Inputs may be any that keep to these rules, and one draw needn't show every extreme that they name: `local_tiles`: entries are 0 or 1. `boundary_tiles`: entries are 0 or 1. `hub_tiles`: entries are 0 or 1. `local_coord`: both columns are row blocks of the same device. `local_count`: some device has all 32 slots live. `hub_coord`: column 0 is a row block below 8, column 1 a hub block below 2.
All inputs are finite; a program needn't handle non-finite values.
Results may differ from a plain program's by a relative error of at most 0.005.
Values may be sent and summed in bfloat16 or wider, within the bound.
A program may use at most 64 MiB of HBM per device.

v0:
```python
import jax
import jax.numpy as jnp
from jax import lax
from jax.sharding import PartitionSpec as P


def tile_sum(tiles, rows, sources, weight, block_count):
    product = jnp.einsum("kij,kjf->kif", tiles, sources, preferred_element_type=jnp.float32)
    onehot = (rows[None, :] == jnp.arange(block_count, dtype=jnp.int32)[:, None]).astype(
        jnp.float32
    ) * weight[None, :]
    flat = product.reshape(product.shape[0], -1)
    merged = jnp.dot(onehot, flat, precision=lax.Precision.HIGHEST)
    return merged.reshape(block_count, product.shape[1], product.shape[2])


def layer(
    nodes_in,
    self_weight,
    neigh_weight,
    degree,
    local_tiles,
    local_coord,
    local_count,
    send_block,
    boundary_tiles,
    boundary_row,
    hub_rows,
    hub_tiles,
    hub_coord,
):
    node_count, feat_width = nodes_in.shape
    tile_size = local_tiles.shape[1]
    block_count = node_count // tile_size
    blocks = nodes_in.reshape(block_count, tile_size, feat_width)
    own_hubs = jnp.take(nodes_in, hub_rows, axis=0)
    inner = lax.all_gather(own_hubs, "gy", axis=0, tiled=True)
    hub_feats = lax.all_gather(inner, "gx", axis=0, tiled=True)
    outgoing = jnp.take(blocks, send_block, axis=0)
    incoming = lax.all_to_all(outgoing, "gy", split_axis=0, concat_axis=0, tiled=True)
    live_mask = (jnp.arange(local_tiles.shape[0], dtype=jnp.int32) < local_count[0]).astype(
        jnp.float32
    )
    sources = jnp.take(blocks, local_coord[:, 1], axis=0)
    totals = tile_sum(local_tiles, local_coord[:, 0], sources, live_mask, block_count)
    totals = totals + tile_sum(
        boundary_tiles,
        boundary_row,
        incoming,
        jnp.ones((boundary_tiles.shape[0],), jnp.float32),
        block_count,
    )
    hub_blocks = hub_feats.reshape(-1, tile_size, feat_width)
    hub_sources = jnp.take(hub_blocks, hub_coord[:, 1], axis=0)
    totals = totals + tile_sum(
        hub_tiles,
        hub_coord[:, 0],
        hub_sources,
        jnp.ones((hub_tiles.shape[0],), jnp.float32),
        block_count,
    )
    neigh = (totals.reshape(node_count, feat_width) / degree[:, None].astype(jnp.float32)).astype(
        jnp.bfloat16
    )
    linear = jnp.dot(nodes_in, self_weight, preferred_element_type=jnp.float32)
    return linear + jnp.dot(neigh, neigh_weight, preferred_element_type=jnp.float32)


def per_device(
    features,
    self_weight_one,
    neigh_weight_one,
    self_weight_two,
    neigh_weight_two,
    degree,
    local_tiles,
    local_coord,
    local_count,
    send_block,
    boundary_tiles,
    boundary_row,
    hub_rows,
    hub_tiles,
    hub_coord,
):
    graph = (
        degree,
        local_tiles,
        local_coord,
        local_count,
        send_block,
        boundary_tiles,
        boundary_row,
        hub_rows,
        hub_tiles,
        hub_coord,
    )
    linear_one = layer(features, self_weight_one, neigh_weight_one, *graph)
    relu_one = jnp.maximum(linear_one, 0.0)
    scale = lax.rsqrt(jnp.mean(relu_one * relu_one, axis=-1, keepdims=True) + 1e-06)
    hidden = (relu_one * scale).astype(jnp.bfloat16)
    linear_two = layer(hidden, self_weight_two, neigh_weight_two, *graph)
    return linear_two.astype(jnp.bfloat16)


def solution(mesh):
    placed = (
        P(("gx", "gy"), None),
        P(),
        P(),
        P(),
        P(),
        P(("gx", "gy")),
        P(("gx", "gy"), None, None),
        P(("gx", "gy"), None),
        P(("gx", "gy")),
        P(("gx", "gy")),
        P(("gx", "gy"), None, None),
        P(("gx", "gy")),
        P(("gx", "gy")),
        P(("gx", "gy"), None, None),
        P(("gx", "gy"), None),
    )
    return jax.shard_map(
        per_device, mesh=mesh, in_specs=placed, out_specs=P(("gx", "gy"), None), check_vma=False
    )
```

profile of v0, /device:TPU:0, one launch (start us, length us, event | category | flops | bytes accessed | tf_op | source)
XLA Modules:
  0.0 126.4 jit_solution(13274462036618419214)
XLA Ops:
  1.5 1.6 %gather_fusion.1 = bf16[8,128,256]{2,1,0:T(8,128)(2,1)S(1)} fusion(bf16[8,128,256]{2,1,0:T(8,128)(2,1)} %bitcast.127, s32[1024]{0:T(1024)S(1)} %pad_clamp_fusion.2), kind=kCustom, calls=%fused_computation.1.clone | custom fusion | bytes 1048608 | tf_op jit(solution)/shard_map/jit(_take)/gather | solution.py:39
  4.3 5.2 %all-to-all-start = ((bf16[8,128,256]{1,2,0:T(8,128)(2,1)}), bf16[8,128,256]{1,2,0:T(8,128)(2,1)S(1)}, u32[]{:S(2)}, u32[]{:S(2)}) async-start(bf16[8,128,256]{1,2,0:T(8,128)(2,1)} %broadcast_select_fusion.1), calls=%async_computation | async-start | bytes 1048576 | tf_op jit(solution)/shard_map/all_to_all | solution.py:40
  10.1 2.0 %gather_fusion = bf16[32,128,256]{2,1,0:T(8,128)(2,1)} fusion(bf16[8,128,256]{2,1,0:T(8,128)(2,1)S(1)} %bitcast.128, s32[1024]{0:T(1024)S(1)} %pad_clamp_fusion.3), kind=kCustom, calls=%fused_computation.clone | custom fusion | bytes 4194432 | tf_op jit(solution)/shard_map/jit(_take)/gather | solution.py:44
  12.2 4.4 %convolution_bitcast_fusion.1 = f32[32,128,256]{1,2,0:T(8,128)} fusion(bf16[32,128,128]{2,1,0:T(8,128)(2,1)S(1)} %copy-done, bf16[32,128,256]{2,1,0:T(8,128)(2,1)} %gather_fusion, pred[32]{0:T(512)(128)(4,1)S(1)} %get-tuple-element.10), kind=kOutput, calls=%fused_computation.15 | convolution fusion | flops 269484032 | bytes 7340064 | tf_op jit(solution)/shard_map/kij,kjf->kif/dot_general | solution.py:8
  16.6 5.4 %copy.38 = f32[4,8,128,256]{3,1,2,0:T(8,128)} copy(f32[4,8,128,256]{2,3,1,0:T(8,128)} %bitcast.130) | data formatting | bytes 8388608
  23.9 9.6 %all_gather.12 = bf16[64,256]{1,0:T(8,128)(2,1)S(1)} all-gather(bf16[8,256]{1,0:T(8,128)(2,1)S(1)} %broadcast_select_fusion.3), channel_id=1, replica_groups=mesh['gx'=4,'gy'=8] {'gy'}, dimensions={0}, use_global_device_ids=true | all-gather | bytes 36864 | tf_op jit(solution)/shard_map/all_gather | solution.py:37
  33.5 13.6 %all_gather.13 = bf16[256,256]{1,0:T(8,128)(2,1)S(1)} all-gather(bf16[64,256]{1,0:T(8,128)(2,1)S(1)} %all_gather.12), channel_id=1, replica_groups=mesh['gx'=4,'gy'=8] {'gx'}, dimensions={0}, use_global_device_ids=true | all-gather | bytes 163840 | tf_op jit(solution)/shard_map/all_gather | solution.py:38
  47.6 1.4 %gather_fusion.3 = bf16[8,128,256]{2,1,0:T(8,128)(2,1)} fusion(bf16[2,128,256]{2,1,0:T(8,128)(2,1)S(1)} %bitcast.135, s32[1024]{0:T(1024)S(1)} %pad_clamp_fusion), kind=kCustom, calls=%fused_computation.3.clone | custom fusion | bytes 1048608 | tf_op jit(solution)/shard_map/jit(_take)/gather | solution.py:54
  49.0 1.5 %convolution_bitcast_fusion.4 = f32[8,128,256]{1,2,0:T(8,128)S(1)} fusion(bf16[8,128,128]{2,1,0:T(8,128)(2,1)} %param.36, bf16[8,128,256]{2,1,0:T(8,128)(2,1)} %gather_fusion.3, pred[8]{0:T(512)(128)(4,1)} %get-tuple-element.6), kind=kOutput, calls=%fused_computation.27 | convolution fusion | flops 67371008 | bytes 1835016 | tf_op jit(solution)/shard_map/kij,kjf->kif/dot_general | solution.py:8
  50.6 1.4 %copy.22 = f32[8,128,256]{2,1,0:T(8,128)} copy(f32[8,128,256]{1,2,0:T(8,128)S(1)} %convolution_bitcast_fusion.4) | data formatting | bytes 2097152 | tf_op jit(solution)/shard_map/kij,kjf->kif/dot_general | solution.py:8
  56.7 2.5 %fusion.35 = f32[8,128,256]{2,0,1:T(8,128)S(1)} fusion(s32[8]{0:T(128)} %param.34, f32[1,8,128,256]{3,2,1,0:T(8,128)} %bitcast.131), kind=kOutput, calls=%fused_computation.64 | convolution fusion | flops 25165888 | bytes 2097184 | tf_op jit(solution)/shard_map/dot_general | solution.py:13
  59.2 3.8 %fusion.10 = f32[8,128,256]{2,0,1:T(8,128)S(1)} fusion(f32[8,128,256]{2,0,1:T(8,128)S(1)} %fusion.35, f32[32]{0:T(128)S(1)} %copy-done.21, s32[32]{0:T(128)S(1)} %copy-done.19, f32[4,8,128,256]{3,1,2,0:T(8,128)} %copy.38), kind=kOutput, calls=%fused_computation.20 | convolution fusion | flops 100925952 | bytes 6291712 | tf_op jit(solution)/shard_map/dot_general | solution.py:13
  65.5 2.0 %gather_fusion.4 = bf16[32,128,256]{2,1,0:T(8,128)(2,1)} fusion(bf16[8,128,256]{2,1,0:T(8,128)(2,1)S(1)} %bitcast.125, s32[1024]{0:T(1024)S(1)} %pad_clamp_fusion.3), kind=kCustom, calls=%fused_computation.4.clone | custom fusion | bytes 4194432 | tf_op jit(solution)/shard_map/jit(_take)/gather | solution.py:44
  68.8 4.4 %convolution_bitcast_fusion = f32[32,128,256]{1,2,0:T(8,128)} fusion(bf16[32,128,128]{2,1,0:T(8,128)(2,1)S(1)} %copy-done, bf16[32,128,256]{2,1,0:T(8,128)(2,1)} %gather_fusion.4, pred[32]{0:T(512)(128)(4,1)S(1)} %copy-done.24), kind=kOutput, calls=%fused_computation.14 | convolution fusion | flops 269484032 | bytes 7340064 | tf_op jit(solution)/shard_map/kij,kjf->kif/dot_general | solution.py:8
  73.3 5.4 %copy.41 = f32[4,8,128,256]{3,1,2,0:T(8,128)} copy(f32[4,8,128,256]{2,3,1,0:T(8,128)} %bitcast.129) | data formatting | bytes 8388608
  79.9 3.5 %all-to-all-start.1 = ((bf16[8,128,256]{1,2,0:T(8,128)(2,1)}), bf16[8,128,256]{1,2,0:T(8,128)(2,1)S(1)}, u32[]{:S(2)}, u32[]{:S(2)}) async-start(bf16[8,128,256]{1,2,0:T(8,128)(2,1)} %broadcast_select_fusion), calls=%async_computation.1 | async-start | bytes 1048576 | tf_op jit(solution)/shard_map/all_to_all | solution.py:40
  83.5 12.9 %all_gather.14 = bf16[64,256]{1,0:T(8,128)(2,1)S(1)} all-gather(bf16[8,256]{1,0:T(8,128)(2,1)S(1)} %broadcast_select_fusion.2), channel_id=1, replica_groups=mesh['gx'=4,'gy'=8] {'gy'}, dimensions={0}, use_global_device_ids=true | all-gather | bytes 36864 | tf_op jit(solution)/shard_map/all_gather | solution.py:37
  96.3 13.6 %all_gather.15 = bf16[256,256]{1,0:T(8,128)(2,1)S(1)} all-gather(bf16[64,256]{1,0:T(8,128)(2,1)S(1)} %all_gather.14), channel_id=1, replica_groups=mesh['gx'=4,'gy'=8] {'gx'}, dimensions={0}, use_global_device_ids=true | all-gather | bytes 163840 | tf_op jit(solution)/shard_map/all_gather | solution.py:38
  109.9 1.4 %gather_fusion.7 = bf16[8,128,256]{2,1,0:T(8,128)(2,1)} fusion(bf16[2,128,256]{2,1,0:T(8,128)(2,1)S(1)} %bitcast.136, s32[1024]{0:T(1024)S(1)} %pad_clamp_fusion), kind=kCustom, calls=%fused_computation.7.clone | custom fusion | bytes 1048608 | tf_op jit(solution)/shard_map/jit(_take)/gather | solution.py:54
  111.3 1.5 %convolution_bitcast_fusion.2 = f32[8,128,256]{1,2,0:T(8,128)S(1)} fusion(bf16[8,128,128]{2,1,0:T(8,128)(2,1)} %param.36, bf16[8,128,256]{2,1,0:T(8,128)(2,1)} %gather_fusion.7, pred[8]{0:T(512)(128)(4,1)} %get-tuple-element.6), kind=kOutput, calls=%fused_computation.23 | convolution fusion | flops 67371008 | bytes 1835016 | tf_op jit(solution)/shard_map/kij,kjf->kif/dot_general | solution.py:8
  112.8 1.3 %copy.30 = f32[8,128,256]{2,1,0:T(8,128)} copy(f32[8,128,256]{1,2,0:T(8,128)S(1)} %convolution_bitcast_fusion.2) | data formatting | bytes 2097152 | tf_op jit(solution)/shard_map/kij,kjf->kif/dot_general | solution.py:8
  114.2 1.3 %fusion.65 = f32[1024,256]{1,0:T(8,128)} fusion(bf16[1024,256]{1,0:T(8,128)(2,1)S(1)} %multiply_convert_fusion, bf16[256,256]{1,0:T(8,128)(2,1)S(1)} %copy-done.9), kind=kOutput, calls=%fused_computation.102 | convolution fusion | flops 134217728 | bytes 1703936 | tf_op jit(solution)/shard_map/dot_general | solution.py:65
  117.1 2.5 %fusion.33 = f32[8,128,256]{2,0,1:T(8,128)S(1)} fusion(s32[8]{0:T(128)S(1)} %copy-done.12, f32[1,8,128,256]{3,2,1,0:T(8,128)} %bitcast.132), kind=kOutput, calls=%fused_computation.63 | convolution fusion | flops 25165888 | bytes 2097184 | tf_op jit(solution)/shard_map/dot_general | solution.py:13
  119.6 3.8 %fusion.13 = f32[8,128,256]{2,0,1:T(8,128)S(1)} fusion(f32[8,128,256]{2,0,1:T(8,128)S(1)} %fusion.33, f32[32]{0:T(128)S(1)} %copy-done.22, s32[32]{0:T(128)S(1)} %copy-done.20, f32[4,8,128,256]{3,1,2,0:T(8,128)} %copy.41), kind=kOutput, calls=%fused_computation.21 | convolution fusion | flops 100925952 | bytes 6291712 | tf_op jit(solution)/shard_map/dot_general | solution.py:13
  (96 shorter events, 19.1 us)
Async XLA Ops:
  0.0 12.2 %copy-start = (bf16[32,128,128]{2,1,0:T(8,128)(2,1)S(1)}, bf16[32,128,128]{2,1,0:T(8,128)(2,1)}, u32[]{:S(2)}) copy-start(bf16[32,128,128]{2,1,0:T(8,128)(2,1)} %param.29) | copy-start | bytes 3145732
  0.0 10.1 %copy-start.1 = (bf16[1024,256]{1,0:T(8,128)(2,1)S(1)}, bf16[1024,256]{1,0:T(8,128)(2,1)}, u32[]{:S(2)}) copy-start(bf16[1024,256]{1,0:T(8,128)(2,1)} %param.23) | copy-start | bytes 1572868
  0.0 9.5 %copy-start.25 = (s32[32,2]{0,1:T(2,128)S(1)}, s32[32,2]{0,1:T(2,128)}, u32[]{:S(2)}) copy-start(s32[32,2]{0,1:T(2,128)} %param.30) | copy-start | bytes 772
  0.0 10.1 %copy-start.27 = (s32[8]{0:T(128)S(1)}, s32[8]{0:T(128)}, u32[]{:S(2)}) copy-start(s32[8]{0:T(128)} %param.35) | copy-start | bytes 100
  4.3 50.8 %all-to-all-start = ((bf16[8,128,256]{1,2,0:T(8,128)(2,1)}), bf16[8,128,256]{1,2,0:T(8,128)(2,1)S(1)}, u32[]{:S(2)}, u32[]{:S(2)}) async-start(bf16[8,128,256]{1,2,0:T(8,128)(2,1)} %broadcast_select_fusion.1), calls=%async_computation | async-start | bytes 1048576 | tf_op jit(solution)/shard_map/all_to_all | solution.py:40
  9.5 7.1 %copy-start.23 = (pred[32]{0:T(512)(128)(4,1)}, pred[32]{0:T(512)(128)(4,1)S(1)}, u32[]{:S(2)}) copy-start(pred[32]{0:T(512)(128)(4,1)S(1)} %get-tuple-element.10) | copy-start | bytes 100
  10.1 13.8 %copy-start.15 = (pred[8]{0:T(512)(128)(4,1)}, pred[8]{0:T(512)(128)(4,1)S(1)}, u32[]{:S(2)}) copy-start(pred[8]{0:T(512)(128)(4,1)S(1)} %compare_and_fusion.1) | copy-start | bytes 28
  16.6 30.5 %copy-start.26 = (s32[8,2]{0,1:T(2,128)S(1)}, s32[8,2]{0,1:T(2,128)}, u32[]{:S(2)}) copy-start(s32[8,2]{0,1:T(2,128)} %param.37) | copy-start | bytes 196
  22.0 31.7 %copy-start.8 = (bf16[256,256]{1,0:T(8,128)(2,1)S(1)}, bf16[256,256]{1,0:T(8,128)(2,1)}, u32[]{:S(2)}) copy-start(bf16[256,256]{1,0:T(8,128)(2,1)} %param.24) | copy-start | bytes 393220
  22.0 33.0 %copy-start.6 = (bf16[8,128,128]{2,1,0:T(8,128)(2,1)S(1)}, bf16[8,128,128]{2,1,0:T(8,128)(2,1)}, u32[]{:S(2)}) copy-start(bf16[8,128,128]{2,1,0:T(8,128)(2,1)} %param.33) | copy-start | bytes 786436
  23.3 27.3 %copy-start.11 = (s32[1024]{0:T(1024)}, s32[1024]{0:T(1024)S(1)}, u32[]{:S(2)}) copy-start(s32[1024]{0:T(1024)S(1)} %pad_clamp_fusion.1) | copy-start | bytes 12292
  55.0 4.1 %copy-start.19 = (s32[32]{0:T(128)S(1)}, s32[32]{0:T(128)}, u32[]{:S(2)}) copy-start(s32[32]{0:T(128)} %slice_bitcast_fusion.1) | copy-start | bytes 388
  55.0 4.1 %copy-start.21 = (f32[32]{0:T(128)S(1)}, f32[32]{0:T(128)}, u32[]{:S(2)}) copy-start(f32[32]{0:T(128)} %compare_convert_fusion) | copy-start | bytes 388
  56.7 6.4 %copy-start.3 = (f32[8,128,256]{2,1,0:T(8,128)S(1)}, f32[8,128,256]{2,1,0:T(8,128)}, u32[]{:S(2)}) copy-start(f32[8,128,256]{2,1,0:T(8,128)} %copy.22) | copy-start | bytes 3145732
  56.7 6.4 %copy-start.17 = (s32[8]{0:T(128)S(1)}, s32[8]{0:T(128)}, u32[]{:S(2)}) copy-start(s32[8]{0:T(128)} %slice_bitcast_fusion) | copy-start | bytes 100
  73.3 5.7 %copy-start.14 = (pred[8]{0:T(512)(128)(4,1)S(1)}, pred[8]{0:T(512)(128)(4,1)}, u32[]{:S(2)}) copy-start(pred[8]{0:T(512)(128)(4,1)} %copy-done.13) | copy-start | bytes 28
  73.3 10.1 %copy-start.16 = (pred[8]{0:T(512)(128)(4,1)S(1)}, pred[8]{0:T(512)(128)(4,1)}, u32[]{:S(2)}) copy-start(pred[8]{0:T(512)(128)(4,1)} %copy-done.15) | copy-start | bytes 28
  78.7 35.5 %copy-start.9 = (bf16[256,256]{1,0:T(8,128)(2,1)S(1)}, bf16[256,256]{1,0:T(8,128)(2,1)}, u32[]{:S(2)}) copy-start(bf16[256,256]{1,0:T(8,128)(2,1)} %param.26) | copy-start | bytes 393220
  79.9 35.6 %all-to-all-start.1 = ((bf16[8,128,256]{1,2,0:T(8,128)(2,1)}), bf16[8,128,256]{1,2,0:T(8,128)(2,1)S(1)}, u32[]{:S(2)}, u32[]{:S(2)}) async-start(bf16[8,128,256]{1,2,0:T(8,128)(2,1)} %broadcast_select_fusion), calls=%async_computation.1 | async-start | bytes 1048576 | tf_op jit(solution)/shard_map/all_to_all | solution.py:40
  112.8 4.3 %copy-start.12 = (s32[8]{0:T(128)S(1)}, s32[8]{0:T(128)}, u32[]{:S(2)}) copy-start(s32[8]{0:T(128)} %param.34) | copy-start | bytes 100
  114.2 5.4 %copy-start.20 = (s32[32]{0:T(128)S(1)}, s32[32]{0:T(128)}, u32[]{:S(2)}) copy-start(s32[32]{0:T(128)} %slice_bitcast_fusion.1) | copy-start | bytes 388
  114.2 5.4 %copy-start.22 = (f32[32]{0:T(128)S(1)}, f32[32]{0:T(128)}, u32[]{:S(2)}) copy-start(f32[32]{0:T(128)} %compare_convert_fusion) | copy-start | bytes 388
  117.1 6.4 %copy-start.2 = (f32[8,128,256]{2,1,0:T(8,128)S(1)}, f32[8,128,256]{2,1,0:T(8,128)}, u32[]{:S(2)}) copy-start(f32[8,128,256]{2,1,0:T(8,128)} %copy.30) | copy-start | bytes 3145732
  117.1 6.4 %copy-start.18 = (s32[8]{0:T(128)S(1)}, s32[8]{0:T(128)}, u32[]{:S(2)}) copy-start(s32[8]{0:T(128)} %slice_bitcast_fusion) | copy-start | bytes 100
  (6 other events, 14.0 us)
where the time goes:
time: 127 us; the launch traced here: 126 us
  blocking collectives  49.6 us (39%)
  matrix products  31.6 us (25%)
  local copies, waits for them, and re-layouts  29.5 us (23%)
  starting transfers between devices  8.67 us (7%)
  other arithmetic  5.83 us (5%)
    all_gather x2, blocking collectives, layer(): hub_feats = lax.all_gather(inner, 'gx', axis=0, tiled=True)  27.1 us
    all_gather x2, blocking collectives, layer(): inner = lax.all_gather(own_hubs, 'gy', axis=0, tiled=True)  22.4 us
    dot_general x6, matrix products, tile_sum(): merged = jnp.dot(onehot, flat, precision=lax.Precision.HIGHEST)  15 us
    dot_general x6, matrix products, tile_sum(): jnp.einsum('kij,kjf->kif', tiles, sources, preferred_element_type=jnp.flo...  12.5 us
    unnamed x58, local copies, waits for them, and re-layouts  11 us
    all_to_all x2, starting transfers between devices, layer(): lax.all_to_all(outgoing, 'gy', split_axis=0, concat_axis=0, tiled=True)  8.67 us
    dot_general x4, local copies, waits for them, and re-layouts, tile_sum(): jnp.einsum('kij,kjf->kif', tiles, sources, preferred_element_type=jnp.flo...  5.27 us
    gather x2, local copies, waits for them, and re-layouts, layer(): sources = jnp.take(blocks, local_coord[:, 1], axis=0)  4.08 us
  transfers between devices with their start and end apart: 2, of which 0 were waited for; matrix products, arithmetic and copies ran while one was open for 22% of the time, Pallas kernels for 0%

commit v1 on v0

v1 whole, which is shorter than its diff:
```python
import functools

import jax
import jax.numpy as jnp
from jax import lax
from jax.experimental import pallas as pl
from jax.experimental.pallas import tpu as pltpu
from jax.sharding import PartitionSpec as P

MESH = pl.DeviceIdType.MESH
GROUP = 8
F32 = jnp.float32
BF16 = jnp.bfloat16


def kernel(
    n_gx,
    n_gy,
    feat,
    ws1,
    wn1,
    ws2,
    wn2,
    deg,
    lcoord,
    lcount,
    send,
    brow,
    hrows,
    hcoord,
    ltiles_any,
    btiles_any,
    htiles_any,
    out_ref,
    ltiles,
    btiles,
    htiles,
    masked,
    gathered,
    hub_src,
    obuf,
    inc,
    hub,
    hub_all,
    hidden,
    acc,
    own_part,
    rdeg,
    tile_sem,
    block_send,
    block_recv,
    row_send,
    row_recv,
    col_send,
    col_recv,
):
    gx = lax.axis_index("gx")
    gy = lax.axis_index("gy")
    blocks, tile, width = feat.shape
    nodes = blocks * tile
    local_groups = ltiles.shape[0] // GROUP
    bound_groups = n_gy // GROUP
    hub_groups = htiles.shape[0] // GROUP
    hub_dev = hrows.shape[0]

    barrier = pltpu.get_barrier_semaphore()
    for k in range(1, n_gy):
        pl.semaphore_signal(
            barrier, inc=1, device_id=(gx, lax.rem(gy + k, n_gy)), device_id_type=MESH
        )
    for k in range(1, n_gx):
        pl.semaphore_signal(
            barrier, inc=1, device_id=(lax.rem(gx + k, n_gx), gy), device_id_type=MESH
        )

    tile_copies = [
        pltpu.make_async_copy(src, dst, tile_sem.at[i])
        for i, (src, dst) in enumerate(
            ((ltiles_any, ltiles), (btiles_any, btiles), (htiles_any, htiles))
        )
    ]
    for copy in tile_copies:
        copy.start()

    def row_copy(layer, k):
        slot = hub.at[layer, gx, gy]
        return pltpu.make_async_remote_copy(
            src_ref=slot,
            dst_ref=slot,
            send_sem=row_send.at[layer, k],
            recv_sem=row_recv.at[layer, k],
            device_id=(gx, lax.rem(gy + k, n_gy)),
            device_id_type=MESH,
        )

    def col_copy(layer, k):
        slot = hub.at[layer, gx]
        return pltpu.make_async_remote_copy(
            src_ref=slot,
            dst_ref=slot,
            send_sem=col_send.at[layer, k],
            recv_sem=col_recv.at[layer, k],
            device_id=(lax.rem(gx + k, n_gx), gy),
            device_id_type=MESH,
        )

    def block_copy(layer, k):
        return pltpu.make_async_remote_copy(
            src_ref=obuf.at[layer, k],
            dst_ref=inc.at[layer, k],
            send_sem=block_send.at[layer, k],
            recv_sem=block_recv.at[layer, k],
            device_id=(gx, lax.rem(gy + k, n_gy)),
            device_id_type=MESH,
        )

    def pick_hubs(layer, src):
        row = lax.broadcasted_iota(jnp.int32, (hub_dev, nodes), 0)
        picked = jnp.zeros((hub_dev, nodes), jnp.int32)
        for k in range(hub_dev):
            picked = jnp.where(row == k, hrows[k], picked)
        col = lax.broadcasted_iota(jnp.int32, (hub_dev, nodes), 1)
        onehot = jnp.where(col == picked, 1.0, 0.0).astype(BF16)
        rows = jnp.dot(onehot, src[...].reshape(nodes, width), preferred_element_type=F32)
        hub[layer, gx, gy] = rows.astype(BF16)

    def fill_blocks(layer, src):
        for k in range(1, n_gy):
            obuf[layer, k] = src[send[lax.rem(gy + k, n_gy)]]
        inc[layer, 0] = src[send[gy]]

    def start_rows(layer):
        for k in range(1, n_gy):
            row_copy(layer, k).start()

    def start_blocks(layer):
        for k in range(1, n_gy):
            block_copy(layer, k).start()

    def pass_rows_on(layer):
        for k in range(1, n_gy):
            row_copy(layer, k).wait_recv()
        for k in range(1, n_gx):
            col_copy(layer, k).start()

    def place(group, u, values, row, live):
        for b in range(blocks):
            weight = jnp.where(jnp.logical_and(row == b, live), 1.0, 0.0).astype(BF16)
            masked[group, b * tile : (b + 1) * tile, u * tile : (u + 1) * tile] = values * weight

    def place_local():
        count = lcount[0]

        def body(g, carry):
            for u in range(GROUP):
                t = g * GROUP + u
                place(g, u, ltiles[t], lcoord[t, 0], t < count)
            return carry

        lax.fori_loop(0, local_groups, body, 0)

    def place_bound():
        def body(g, carry):
            for u in range(GROUP):
                p = lax.rem(gy + n_gy - (g * GROUP + u), n_gy)
                place(local_groups + g, u, btiles[p], brow[p], True)
            return carry

        lax.fori_loop(0, bound_groups, body, 0)

    def place_hub():
        def body(g, carry):
            for u in range(GROUP):
                t = g * GROUP + u
                place(local_groups + bound_groups + g, u, htiles[t], hcoord[t, 0], True)
            return carry

        lax.fori_loop(0, hub_groups, body, 0)

    def local_work(src, self_weight):
        own_part[...] = jnp.dot(
            src[...].reshape(nodes, width), self_weight[...], preferred_element_type=F32
        )
        acc[...] = jnp.zeros_like(acc)

        def body(g, carry):
            for u in range(GROUP):
                gathered[u * tile : (u + 1) * tile, :] = src[lcoord[g * GROUP + u, 1]]
            acc[...] += jnp.dot(masked[g], gathered[...], preferred_element_type=F32)
            return carry

        lax.fori_loop(0, local_groups, body, 0)

    def remote_work(layer):
        for k in range(1, n_gx):
            col_copy(layer, k).wait_recv()
        hub_all[...] = (
            hub[layer].astype(F32).reshape(hub_all.shape).astype(BF16)
        )

        def hub_body(g, carry):
            for u in range(GROUP):
                hub_src[u * tile : (u + 1) * tile, :] = hub_all[hcoord[g * GROUP + u, 1]]
            acc[...] += jnp.dot(
                masked[local_groups + bound_groups + g],
                hub_src[...],
                preferred_element_type=F32,
            )
            return carry

        lax.fori_loop(0, hub_groups, hub_body, 0)

        for g in range(bound_groups):
            for k in range(g * GROUP, (g + 1) * GROUP):
                if k:
                    block_copy(layer, k).wait_recv()
            acc[...] += jnp.dot(
                masked[local_groups + g],
                inc[layer, g * GROUP : (g + 1) * GROUP].reshape(GROUP * tile, width),
                preferred_element_type=F32,
            )

    def combine(b, neigh_weight):
        rows = slice(2 * b * tile, 2 * (b + 1) * tile)
        inverse = rdeg[rows, :]
        neigh = (acc[rows, :] * jnp.concatenate([inverse, inverse], axis=1)).astype(BF16)
        return own_part[rows, :] + jnp.dot(
            neigh, neigh_weight[...], preferred_element_type=F32
        )

    pick_hubs(0, feat)
    fill_blocks(0, feat)
    pl.semaphore_wait(barrier, n_gy - 1 + n_gx - 1)
    start_rows(0)
    start_blocks(0)
    for b in range(blocks):
        inverse = 1.0 / deg[b : b + 1, :].astype(F32)
        rdeg[b * tile : (b + 1) * tile, :] = jnp.broadcast_to(inverse, (tile, tile)).T
    tile_copies[1].wait()
    place_bound()
    pass_rows_on(0)
    tile_copies[2].wait()
    place_hub()
    tile_copies[0].wait()
    place_local()
    local_work(feat, ws1)
    remote_work(0)
    for b in range(blocks // 2):
        linear = jnp.maximum(combine(b, wn1), 0.0)
        scale = lax.rsqrt(jnp.mean(linear * linear, axis=-1, keepdims=True) + 1e-06)
        hidden[2 * b : 2 * b + 2] = (linear * scale).astype(BF16).reshape(2, tile, width)

    pick_hubs(1, hidden)
    start_rows(1)
    fill_blocks(1, hidden)
    start_blocks(1)
    local_work(hidden, ws2)
    pass_rows_on(1)
    remote_work(1)
    for b in range(blocks // 2):
        out_ref[2 * b : 2 * b + 2] = combine(b, wn2).astype(BF16).reshape(2, tile, width)

    for layer in range(2):
        for k in range(1, n_gy):
            row_copy(layer, k).wait_send()
            block_copy(layer, k).wait_send()
        for k in range(1, n_gx):
            col_copy(layer, k).wait_send()


def per_device(
    n_gx,
    n_gy,
    features,
    self_weight_one,
    neigh_weight_one,
    self_weight_two,
    neigh_weight_two,
    degree,
    local_tiles,
    local_coord,
    local_count,
    send_block,
    boundary_tiles,
    boundary_row,
    hub_rows,
    hub_tiles,
    hub_coord,
):
    nodes, width = features.shape
    tile = local_tiles.shape[1]
    blocks = nodes // tile
    hub_dev = hub_rows.shape[0]
    hub_blocks = n_gx * n_gy * hub_dev // tile
    groups = (local_tiles.shape[0] + n_gy + hub_tiles.shape[0]) // GROUP
    vmem = pl.BlockSpec(memory_space=pltpu.VMEM)
    smem = pl.BlockSpec(memory_space=pltpu.SMEM)
    anywhere = pl.BlockSpec(memory_space=pl.ANY)
    dma = pltpu.SemaphoreType.DMA
    out = pl.pallas_call(
        functools.partial(kernel, n_gx, n_gy),
        out_shape=jax.ShapeDtypeStruct((blocks, tile, width), BF16),
        in_specs=[vmem] * 6 + [smem] * 6 + [anywhere] * 3,
        out_specs=vmem,
        scratch_shapes=[
            pltpu.VMEM(local_tiles.shape, BF16),
            pltpu.VMEM(boundary_tiles.shape, BF16),
            pltpu.VMEM(hub_tiles.shape, BF16),
            pltpu.VMEM((groups, nodes, GROUP * tile), BF16),
            pltpu.VMEM((GROUP * tile, width), BF16),
            pltpu.VMEM((GROUP * tile, width), BF16),
            pltpu.VMEM((2, n_gy, tile, width), BF16),
            pltpu.VMEM((2, n_gy, tile, width), BF16),
            pltpu.VMEM((2, n_gx, n_gy, hub_dev, width), BF16),
            pltpu.VMEM((hub_blocks, tile, width), BF16),
            pltpu.VMEM((blocks, tile, width), BF16),
            pltpu.VMEM((nodes, width), F32),
            pltpu.VMEM((nodes, width), F32),
            pltpu.VMEM((nodes, tile), F32),
            dma((3,)),
            dma((2, n_gy)),
            dma((2, n_gy)),
            dma((2, n_gy)),
            dma((2, n_gy)),
            dma((2, n_gx)),
            dma((2, n_gx)),
        ],
        compiler_params=pltpu.CompilerParams(
            collective_id=0, has_side_effects=True, vmem_limit_bytes=56 * 2**20
        ),
        name="sage_two_layers",
    )(
        features.reshape(blocks, tile, width),
        self_weight_one,
        neigh_weight_one,
        self_weight_two,
        neigh_weight_two,
        degree.reshape(blocks, tile),
        local_coord,
        local_count,
        send_block,
        boundary_row,
        hub_rows,
        hub_coord,
        local_tiles,
        boundary_tiles,
        hub_tiles,
    )
    return out.reshape(nodes, width)


def solution(mesh):
    placed = (
        P(("gx", "gy"), None),
        P(),
        P(),
        P(),
        P(),
        P(("gx", "gy")),
        P(("gx", "gy"), None, None),
        P(("gx", "gy"), None),
        P(("gx", "gy")),
        P(("gx", "gy")),
        P(("gx", "gy"), None, None),
        P(("gx", "gy")),
        P(("gx", "gy")),
        P(("gx", "gy"), None, None),
        P(("gx", "gy"), None),
    )
    return jax.shard_map(
        functools.partial(per_device, mesh.shape["gx"], mesh.shape["gy"]),
        mesh=mesh,
        in_specs=placed,
        out_specs=P(("gx", "gy"), None),
        check_vma=False,
    )
```

time: 127 us -> 36.9 us (0.29)
  blocking collectives: 49.6 us -> 0 us
  Pallas kernels: 0 us -> 32.1 us
  matrix products: 31.6 us -> 0 us
  local copies, waits for them, and re-layouts: 29.5 us -> 3.91 us
  starting transfers between devices: 8.67 us -> 0 us
  other arithmetic: 5.83 us -> 0 us
    all_gather x4 -> x0, blocking collectives: 49.6 us -> none  [the longest x2 27.1 us: layer(): hub_feats = lax.all_gather(inner, 'gx', axis=0, tiled=True)]
    pallas_call x0 -> x1, Pallas kernels: none -> 32.1 us  [per_device(): pl.pallas_call(functools.partial(kernel, n_gx, n_gy), out_shape=jax.Shape...]
    dot_general x16 -> x0, matrix products: 31.6 us -> none  [the longest x6 15 us: tile_sum(): merged = jnp.dot(onehot, flat, precision=lax.Precision.HIGHEST)]
    gather x10 -> x0, local copies, waits for them, and re-layouts: 10.9 us -> none  [the longest x2 4.08 us: layer(): sources = jnp.take(blocks, local_coord[:, 1], axis=0)]
    all_to_all x2 -> x0, starting transfers between devices: 8.67 us -> none  [layer(): lax.all_to_all(outgoing, 'gy', split_axis=0, concat_axis=0, tiled=True)]
    unnamed x58 -> x7, local copies, waits for them, and re-layouts: 11 us -> 3.91 us
    dot_general x4 -> x0, local copies, waits for them, and re-layouts: 5.27 us -> none  [tile_sum(): jnp.einsum('kij,kjf->kif', tiles, sources, preferred_element_type=jnp.flo...]
    select_n x6 -> x0, other arithmetic: 2.75 us -> none  [the longest x3 2.6 us: layer(): outgoing = jnp.take(blocks, send_block, axis=0)]
  transfers between devices with their start and end apart: 2 -> 0, of which waited for: 0 -> 0; matrix products, arithmetic and copies ran while one was open for 22% -> 0% of each run, Pallas kernels for 0% -> 0%
where the time goes in v1:
time: 36.9 us; the launch traced here: 36.6 us
  Pallas kernels  32.1 us (87%)
  local copies, waits for them, and re-layouts  3.91 us (11%)
  between operations  0.67 us (2%)
    pallas_call x1, Pallas kernels, per_device(): pl.pallas_call(functools.partial(kernel, n_gx, n_gy), out_shape=jax.Shape...  32.1 us
    unnamed x7, local copies, waits for them, and re-layouts  3.91 us

profile of v1, /device:TPU:0, one launch (start us, length us, event | category | flops | bytes accessed | tf_op | source)
XLA Modules:
  0.0 36.6 jit_solution(17705098111243855865)
XLA Ops:
  0.7 0.0 copy-start
  0.7 0.7 %copy-done = s32[8,2]{0,1:T(2,128)S(1)} copy-done((s32[8,2]{0,1:T(2,128)S(1)}, s32[8,2]{0,1:T(2,128)}, u32[]{:S(2)}) %copy-start) | copy-done | bytes 88
  1.3 0.0 copy-start.1
  1.3 0.7 %copy.17.hcoord = s32[8,2]{1,0:T(8,128)} copy(s32[8,2]{0,1:T(2,128)S(1)} %copy-done) | data formatting | bytes 128 | tf_op args[14]
  2.0 0.0 copy-done.1
  2.0 0.7 %copy.16.lcoord = s32[32,2]{1,0:T(8,128)} copy(s32[32,2]{0,1:T(2,128)S(1)} %copy-done.1) | data formatting | bytes 512 | tf_op args[7]
  2.7 32.1 %sage_two_layers.1 = bf16[8,128,256]{2,1,0:T(8,128)(2,1)} custom-call(bf16[8,128,256]{2,1,0:T(8,128)(2,1)} %bitcast.4, bf16[256,256]{1,0:T(8,128)(2,1)} %ws1.1, bf16[256,256]{1,0:T(8,128)(2,1)} %wn1.1, bf16[256,256]{1,0:T(8,128)(2,1)} %ws2.1, bf16[256,256]{1,0:T(8,128)(2,1)} %wn2.1, s32[8,128]{1,0:T(8,128)} %bitcast.5, s32[32,2]{1,0:T(8,128)} %copy.16.lcoord, ...), custom_call_target="tpu_custom_call" | custom-call | tf_op jit(solution)/shard_map/sage_two_layers/pallas_call | solution.py:300
  34.8 1.9 %copy.20 = bf16[1024,256]{1,0:T(8,128)(2,1)} copy(bf16[1024,256]{1,0:T(8,128)(2,1)} %bitcast.3) | data formatting | bytes 1048576
Async XLA Ops:
  0.7 0.7 %copy-start = (s32[8,2]{0,1:T(2,128)S(1)}, s32[8,2]{0,1:T(2,128)}, u32[]{:S(2)}) copy-start(s32[8,2]{0,1:T(2,128)} %param.29) | copy-start | bytes 196
  1.3 0.7 %copy-start.1 = (s32[32,2]{0,1:T(2,128)S(1)}, s32[32,2]{0,1:T(2,128)}, u32[]{:S(2)}) copy-start(s32[32,2]{0,1:T(2,128)} %param.22) | copy-start | bytes 772

commit v2 on v1

--- a/solution.py
+++ b/solution.py
@@ -16,11 +16,6 @@
 def kernel(
     n_gx,
     n_gy,
-    feat,
-    ws1,
-    wn1,
-    ws2,
-    wn2,
     deg,
     lcoord,
     lcount,
@@ -28,13 +23,24 @@
     brow,
     hrows,
     hcoord,
+    feat_any,
+    ws1_any,
+    wn1_any,
+    ws2_any,
+    wn2_any,
     ltiles_any,
     btiles_any,
     htiles_any,
     out_ref,
+    feat,
+    ws1,
+    wn1,
+    ws2,
+    wn2,
     ltiles,
     btiles,
     htiles,
+    wide,
     masked,
     gathered,
     hub_src,
@@ -46,7 +52,7 @@
     acc,
     own_part,
     rdeg,
-    tile_sem,
+    load_sem,
     block_send,
     block_recv,
     row_send,
@@ -63,24 +69,40 @@
     hub_groups = htiles.shape[0] // GROUP
     hub_dev = hrows.shape[0]
 
+    def peer(k):
+        place, other = 1, 0
+        while place < n_gy:
+            other += lax.rem(lax.div(gy, place) + lax.div(k, place), 2) * place
+            place *= 2
+        return other
+
     barrier = pltpu.get_barrier_semaphore()
     for k in range(1, n_gy):
         pl.semaphore_signal(
-            barrier, inc=1, device_id=(gx, lax.rem(gy + k, n_gy)), device_id_type=MESH
+            barrier, inc=1, device_id=(gx, peer(k)), device_id_type=MESH
         )
     for k in range(1, n_gx):
         pl.semaphore_signal(
             barrier, inc=1, device_id=(lax.rem(gx + k, n_gx), gy), device_id_type=MESH
         )
 
-    tile_copies = [
-        pltpu.make_async_copy(src, dst, tile_sem.at[i])
+    loads = [
+        pltpu.make_async_copy(src, dst, load_sem.at[i])
         for i, (src, dst) in enumerate(
-            ((ltiles_any, ltiles), (btiles_any, btiles), (htiles_any, htiles))
+            (
+                (feat_any, feat),
+                (btiles_any, btiles),
+                (htiles_any, htiles),
+                (ltiles_any, ltiles),
+                (ws1_any, ws1),
+                (wn1_any, wn1),
+                (ws2_any, ws2),
+                (wn2_any, wn2),
+            )
         )
     ]
-    for copy in tile_copies:
-        copy.start()
+    for load in loads:
+        load.start()
 
     def row_copy(layer, k):
         slot = hub.at[layer, gx, gy]
@@ -89,7 +111,7 @@
             dst_ref=slot,
             send_sem=row_send.at[layer, k],
             recv_sem=row_recv.at[layer, k],
-            device_id=(gx, lax.rem(gy + k, n_gy)),
+            device_id=(gx, peer(k)),
             device_id_type=MESH,
         )
 
@@ -110,23 +132,21 @@
             dst_ref=inc.at[layer, k],
             send_sem=block_send.at[layer, k],
             recv_sem=block_recv.at[layer, k],
-            device_id=(gx, lax.rem(gy + k, n_gy)),
+            device_id=(gx, peer(k)),
             device_id_type=MESH,
         )
 
-    def pick_hubs(layer, src):
-        row = lax.broadcasted_iota(jnp.int32, (hub_dev, nodes), 0)
-        picked = jnp.zeros((hub_dev, nodes), jnp.int32)
+    def pick_hubs(layer):
+        row = lax.broadcasted_iota(jnp.int32, (hub_dev, width), 0)
+        rows = jnp.zeros((hub_dev, width), F32)
         for k in range(hub_dev):
-            picked = jnp.where(row == k, hrows[k], picked)
-        col = lax.broadcasted_iota(jnp.int32, (hub_dev, nodes), 1)
-        onehot = jnp.where(col == picked, 1.0, 0.0).astype(BF16)
-        rows = jnp.dot(onehot, src[...].reshape(nodes, width), preferred_element_type=F32)
+            value = jnp.broadcast_to(wide[pl.ds(hrows[k], 1), :], (hub_dev, width))
+            rows = jnp.where(row == k, value, rows)
         hub[layer, gx, gy] = rows.astype(BF16)
 
     def fill_blocks(layer, src):
         for k in range(1, n_gy):
-            obuf[layer, k] = src[send[lax.rem(gy + k, n_gy)]]
+            obuf[layer, k] = src[send[peer(k)]]
         inc[layer, 0] = src[send[gy]]
 
     def start_rows(layer):
@@ -154,7 +174,7 @@
         def body(g, carry):
             for u in range(GROUP):
                 t = g * GROUP + u
-                place(g, u, ltiles[t], lcoord[t, 0], t < count)
+                place(g, u, ltiles[t], lcoord[0, t], t < count)
             return carry
 
         lax.fori_loop(0, local_groups, body, 0)
@@ -162,7 +182,7 @@
     def place_bound():
         def body(g, carry):
             for u in range(GROUP):
-                p = lax.rem(gy + n_gy - (g * GROUP + u), n_gy)
+                p = peer(g * GROUP + u)
                 place(local_groups + g, u, btiles[p], brow[p], True)
             return carry
 
@@ -172,35 +192,49 @@
         def body(g, carry):
             for u in range(GROUP):
                 t = g * GROUP + u
-                place(local_groups + bound_groups + g, u, htiles[t], hcoord[t, 0], True)
+                place(local_groups + bound_groups + g, u, htiles[t], hcoord[0, t], True)
             return carry
 
         lax.fori_loop(0, hub_groups, body, 0)
 
-    def local_work(src, self_weight):
+    def local_first(src, self_weight):
         own_part[...] = jnp.dot(
             src[...].reshape(nodes, width), self_weight[...], preferred_element_type=F32
         )
-        acc[...] = jnp.zeros_like(acc)
-
+        acc[...] = local_sum(src, 0)
+
+    def local_sum(src, g):
+        for u in range(GROUP):
+            gathered[u * tile : (u + 1) * tile, :] = src[lcoord[1, g * GROUP + u]]
+        return jnp.dot(masked[g], gathered[...], preferred_element_type=F32)
+
+    def local_rest(src):
         def body(g, carry):
-            for u in range(GROUP):
-                gathered[u * tile : (u + 1) * tile, :] = src[lcoord[g * GROUP + u, 1]]
-            acc[...] += jnp.dot(masked[g], gathered[...], preferred_element_type=F32)
+            acc[...] += local_sum(src, g)
             return carry
 
-        lax.fori_loop(0, local_groups, body, 0)
+        lax.fori_loop(1, local_groups, body, 0)
+
+    def bound_sum(layer, rows, start, stop):
+        first = (bound_groups - 1) * GROUP
+        return jnp.dot(
+            masked[local_groups + bound_groups - 1, rows, start * tile : stop * tile],
+            inc[layer, first + start : first + stop].reshape((stop - start) * tile, width),
+            preferred_element_type=F32,
+        )
+
+    def wait_blocks(layer, start, stop):
+        for k in range(max(start, 1), stop):
+            block_copy(layer, k).wait_recv()
 
     def remote_work(layer):
         for k in range(1, n_gx):
             col_copy(layer, k).wait_recv()
-        hub_all[...] = (
-            hub[layer].astype(F32).reshape(hub_all.shape).astype(BF16)
-        )
+        hub_all[...] = hub[layer].astype(F32).reshape(hub_all.shape).astype(BF16)
 
         def hub_body(g, carry):
             for u in range(GROUP):
-                hub_src[u * tile : (u + 1) * tile, :] = hub_all[hcoord[g * GROUP + u, 1]]
+                hub_src[u * tile : (u + 1) * tile, :] = hub_all[hcoord[1, g * GROUP + u]]
             acc[...] += jnp.dot(
                 masked[local_groups + bound_groups + g],
                 hub_src[...],
@@ -210,55 +244,65 @@
 
         lax.fori_loop(0, hub_groups, hub_body, 0)
 
-        for g in range(bound_groups):
-            for k in range(g * GROUP, (g + 1) * GROUP):
-                if k:
-                    block_copy(layer, k).wait_recv()
+        for g in range(bound_groups - 1):
+            wait_blocks(layer, g * GROUP, (g + 1) * GROUP)
             acc[...] += jnp.dot(
                 masked[local_groups + g],
                 inc[layer, g * GROUP : (g + 1) * GROUP].reshape(GROUP * tile, width),
                 preferred_element_type=F32,
             )
-
-    def combine(b, neigh_weight):
+        every = slice(0, nodes)
+        wait_blocks(layer, n_gy - 8, n_gy - 4)
+        acc[...] += bound_sum(layer, every, 0, 4)
+        wait_blocks(layer, n_gy - 4, n_gy - 2)
+        acc[...] += bound_sum(layer, every, 4, 6)
+        wait_blocks(layer, n_gy - 2, n_gy)
+
+    def combine(layer, b, neigh_weight):
         rows = slice(2 * b * tile, 2 * (b + 1) * tile)
         inverse = rdeg[rows, :]
-        neigh = (acc[rows, :] * jnp.concatenate([inverse, inverse], axis=1)).astype(BF16)
+        total = acc[rows, :] + bound_sum(layer, rows, 6, 8)
+        neigh = (total * jnp.concatenate([inverse, inverse], axis=1)).astype(BF16)
         return own_part[rows, :] + jnp.dot(
             neigh, neigh_weight[...], preferred_element_type=F32
         )
 
-    pick_hubs(0, feat)
+    loads[0].wait()
     fill_blocks(0, feat)
+    wide[...] = feat[...].reshape(nodes, width).astype(F32)
+    pick_hubs(0)
     pl.semaphore_wait(barrier, n_gy - 1 + n_gx - 1)
     start_rows(0)
     start_blocks(0)
     for b in range(blocks):
         inverse = 1.0 / deg[b : b + 1, :].astype(F32)
         rdeg[b * tile : (b + 1) * tile, :] = jnp.broadcast_to(inverse, (tile, tile)).T
-    tile_copies[1].wait()
+    for load in loads[1:]:
+        load.wait()
     place_bound()
+    place_hub()
     pass_rows_on(0)
-    tile_copies[2].wait()
-    place_hub()
-    tile_copies[0].wait()
     place_local()
-    local_work(feat, ws1)
+    local_first(feat, ws1)
+    local_rest(feat)
     remote_work(0)
     for b in range(blocks // 2):
-        linear = jnp.maximum(combine(b, wn1), 0.0)
+        linear = jnp.maximum(combine(0, b, wn1), 0.0)
         scale = lax.rsqrt(jnp.mean(linear * linear, axis=-1, keepdims=True) + 1e-06)
-        hidden[2 * b : 2 * b + 2] = (linear * scale).astype(BF16).reshape(2, tile, width)
-
-    pick_hubs(1, hidden)
+        normed = linear * scale
+        wide[2 * b * tile : 2 * (b + 1) * tile, :] = normed
+        hidden[2 * b : 2 * b + 2] = normed.astype(BF16).reshape(2, tile, width)
+
+    pick_hubs(1)
     start_rows(1)
     fill_blocks(1, hidden)
     start_blocks(1)
-    local_work(hidden, ws2)
+    local_first(hidden, ws2)
     pass_rows_on(1)
+    local_rest(hidden)
     remote_work(1)
     for b in range(blocks // 2):
-        out_ref[2 * b : 2 * b + 2] = combine(b, wn2).astype(BF16).reshape(2, tile, width)
+        out_ref[2 * b : 2 * b + 2] = combine(1, b, wn2).astype(BF16).reshape(2, tile, width)
 
     for layer in range(2):
         for k in range(1, n_gy):
@@ -266,6 +310,16 @@
             block_copy(layer, k).wait_send()
         for k in range(1, n_gx):
             col_copy(layer, k).wait_send()
+
+
+def store_kernel(src, dst, sem):
+    copies = [
+        pltpu.make_async_copy(src.at[b], dst.at[b], sem.at[b]) for b in range(src.shape[0])
+    ]
+    for copy in copies:
+        copy.start()
+    for copy in copies:
+        copy.wait()
 
 
 def per_device(
@@ -300,12 +354,18 @@
     out = pl.pallas_call(
         functools.partial(kernel, n_gx, n_gy),
         out_shape=jax.ShapeDtypeStruct((blocks, tile, width), BF16),
-        in_specs=[vmem] * 6 + [smem] * 6 + [anywhere] * 3,
+        in_specs=[vmem] + [smem] * 6 + [anywhere] * 8,
         out_specs=vmem,
         scratch_shapes=[
+            pltpu.VMEM((blocks, tile, width), BF16),
+            pltpu.VMEM((width, width), BF16),
+            pltpu.VMEM((width, width), BF16),
+            pltpu.VMEM((width, width), BF16),
+            pltpu.VMEM((width, width), BF16),
             pltpu.VMEM(local_tiles.shape, BF16),
             pltpu.VMEM(boundary_tiles.shape, BF16),
             pltpu.VMEM(hub_tiles.shape, BF16),
+            pltpu.VMEM((nodes, width), F32),
             pltpu.VMEM((groups, nodes, GROUP * tile), BF16),
             pltpu.VMEM((GROUP * tile, width), BF16),
             pltpu.VMEM((GROUP * tile, width), BF16),
@@ -317,7 +377,7 @@
             pltpu.VMEM((nodes, width), F32),
             pltpu.VMEM((nodes, width), F32),
             pltpu.VMEM((nodes, tile), F32),
-            dma((3,)),
+            dma((8,)),
             dma((2, n_gy)),
             dma((2, n_gy)),
             dma((2, n_gy)),
@@ -330,22 +390,30 @@
         ),
         name="sage_two_layers",
     )(
+        degree.reshape(blocks, tile),
+        local_coord.T,
+        local_count,
+        send_block,
+        boundary_row,
+        hub_rows,
+        hub_coord.T,
         features.reshape(blocks, tile, width),
         self_weight_one,
         neigh_weight_one,
         self_weight_two,
         neigh_weight_two,
-        degree.reshape(blocks, tile),
-        local_coord,
-        local_count,
-        send_block,
-        boundary_row,
-        hub_rows,
-        hub_coord,
         local_tiles,
         boundary_tiles,
         hub_tiles,
     )
+    out = pl.pallas_call(
+        store_kernel,
+        out_shape=jax.ShapeDtypeStruct((blocks, tile, width), BF16),
+        in_specs=[anywhere],
+        out_specs=anywhere,
+        scratch_shapes=[dma((blocks,))],
+        name="store_result",
+    )(out)
     return out.reshape(nodes, width)
 
 

time: 36.9 us -> 46.9 us (1.27)
  Pallas kernels: 32.1 us -> 46 us
  local copies, waits for them, and re-layouts: 3.91 us -> 0 us
    pallas_call x0 -> x1, Pallas kernels: none -> 17.1 us  [per_device(): pl.pallas_call(store_kernel, out_shape=jax.ShapeDtypeStruct((blocks, tile...]
    unnamed x7 -> x0, local copies, waits for them, and re-layouts: 3.91 us -> none
    pallas_call x1, Pallas kernels: 32.1 us -> 29 us  [per_device(): pl.pallas_call(functools.partial(kernel, n_gx, n_gy), out_shape=jax.Shape...]
where the time goes in v2:
time: 46.9 us; the launch traced here: 46.7 us
  Pallas kernels  46 us (98%)
  between operations  0.66 us (1%)
    pallas_call x1, Pallas kernels, per_device(): pl.pallas_call(functools.partial(kernel, n_gx, n_gy), out_shape=jax.Shape...  29 us
    pallas_call x1, Pallas kernels, per_device(): pl.pallas_call(store_kernel, out_shape=jax.ShapeDtypeStruct((blocks, tile...  17.1 us

profile of v2, /device:TPU:0, one launch (start us, length us, event | category | flops | bytes accessed | tf_op | source)
XLA Modules:
  0.0 46.7 jit_solution(10057907282559291282)
XLA Ops:
  0.7 29.0 %sage_two_layers.1.src = bf16[8,128,256]{2,1,0:T(8,128)(2,1)} custom-call(s32[8,128]{1,0:T(8,128)} %bitcast.6, s32[2,32]{1,0:T(2,128)} %bitcast.7, s32[1]{0:T(128)S(6)} %copy.16.lcount, s32[8]{0:T(128)} %send.1, s32[8]{0:T(128)} %brow.1, s32[8]{0:T(128)} %hrows.1, s32[2,8]{1,0:T(2,128)} %bitcast.8, bf16[8,128,256]{2,1,0:T(8,128)(2,1)} %bitcast.5, ...), custom_call_target="tpu_custom_call" | custom-call | tf_op jit(solution)/shard_map/sage_two_layers/pallas_call | solution.py:354
  29.6 17.1 %store_result.1 = bf16[8,128,256]{2,1,0:T(8,128)(2,1)} custom-call(bf16[8,128,256]{2,1,0:T(8,128)(2,1)} %sage_two_layers.1.src), custom_call_target="tpu_custom_call" | custom-call | tf_op jit(solution)/shard_map/store_result/pallas_call | solution.py:409

commit v3 on v2

--- a/solution.py
+++ b/solution.py
@@ -312,14 +312,20 @@
             col_copy(layer, k).wait_send()
 
 
-def store_kernel(src, dst, sem):
-    copies = [
-        pltpu.make_async_copy(src.at[b], dst.at[b], sem.at[b]) for b in range(src.shape[0])
+def store_kernel(src, dst, held, load_sem, store_sem):
+    loads = [
+        pltpu.make_async_copy(src.at[b], held.at[b], load_sem.at[b]) for b in range(src.shape[0])
     ]
-    for copy in copies:
-        copy.start()
-    for copy in copies:
-        copy.wait()
+    stores = [
+        pltpu.make_async_copy(held.at[b], dst.at[b], store_sem.at[b]) for b in range(src.shape[0])
+    ]
+    for load in loads:
+        load.start()
+    for load, store in zip(loads, stores):
+        load.wait()
+        store.start()
+    for store in stores:
+        store.wait()
 
 
 def per_device(
@@ -411,7 +417,11 @@
         out_shape=jax.ShapeDtypeStruct((blocks, tile, width), BF16),
         in_specs=[anywhere],
         out_specs=anywhere,
-        scratch_shapes=[dma((blocks,))],
+        scratch_shapes=[
+            pltpu.VMEM((blocks, tile, width), BF16),
+            dma((blocks,)),
+            dma((blocks,)),
+        ],
         name="store_result",
     )(out)
     return out.reshape(nodes, width)

time: 46.9 us -> 31.7 us (0.68)
  Pallas kernels: 46 us -> 30.8 us
    pallas_call x1, Pallas kernels: 17.1 us -> 1.83 us  [per_device(): pl.pallas_call(store_kernel, out_shape=jax.ShapeDtypeStruct((blocks, tile...]
where the time goes in v3:
time: 31.7 us; the launch traced here: 31.5 us
  Pallas kernels  30.8 us (97%)
  between operations  0.66 us (2%)
    pallas_call x1, Pallas kernels, per_device(): pl.pallas_call(functools.partial(kernel, n_gx, n_gy), out_shape=jax.Shape...  29 us
    pallas_call x1, Pallas kernels, per_device(): pl.pallas_call(store_kernel, out_shape=jax.ShapeDtypeStruct((blocks, tile...  1.83 us

profile of v3, /device:TPU:0, one launch (start us, length us, event | category | flops | bytes accessed | tf_op | source)
XLA Modules:
  0.0 31.5 jit_solution(11061925291662553643)
XLA Ops:
  0.7 29.0 %sage_two_layers.1.src = bf16[8,128,256]{2,1,0:T(8,128)(2,1)} custom-call(s32[8,128]{1,0:T(8,128)} %bitcast.6, s32[2,32]{1,0:T(2,128)} %bitcast.7, s32[1]{0:T(128)S(6)} %copy.16.lcount, s32[8]{0:T(128)} %send.1, s32[8]{0:T(128)} %brow.1, s32[8]{0:T(128)} %hrows.1, s32[2,8]{1,0:T(2,128)} %bitcast.8, bf16[8,128,256]{2,1,0:T(8,128)(2,1)} %bitcast.5, ...), custom_call_target="tpu_custom_call" | custom-call | tf_op jit(solution)/shard_map/sage_two_layers/pallas_call | solution.py:360
  29.6 1.8 %store_result.1 = bf16[8,128,256]{2,1,0:T(8,128)(2,1)} custom-call(bf16[8,128,256]{2,1,0:T(8,128)(2,1)} %sage_two_layers.1.src), custom_call_target="tpu_custom_call" | custom-call | tf_op jit(solution)/shard_map/store_result/pallas_call | solution.py:415

commit v4 on v3

--- a/solution.py
+++ b/solution.py
@@ -163,45 +163,41 @@
         for k in range(1, n_gx):
             col_copy(layer, k).start()
 
-    def place(group, u, values, row, live):
+    def place(first, t, values, row, live):
+        group = first + lax.div(t, GROUP)
+        columns = pl.ds(pl.multiple_of(lax.rem(t, GROUP) * tile, tile), tile)
         for b in range(blocks):
             weight = jnp.where(jnp.logical_and(row == b, live), 1.0, 0.0).astype(BF16)
-            masked[group, b * tile : (b + 1) * tile, u * tile : (u + 1) * tile] = values * weight
+            masked[group, b * tile : (b + 1) * tile, columns] = values * weight
 
     def place_local():
         count = lcount[0]
 
-        def body(g, carry):
-            for u in range(GROUP):
-                t = g * GROUP + u
-                place(g, u, ltiles[t], lcoord[0, t], t < count)
+        def body(t, carry):
+            place(0, t, ltiles[t], lcoord[0, t], t < count)
             return carry
 
-        lax.fori_loop(0, local_groups, body, 0)
+        lax.fori_loop(0, local_groups * GROUP, body, 0)
 
     def place_bound():
-        def body(g, carry):
-            for u in range(GROUP):
-                p = peer(g * GROUP + u)
-                place(local_groups + g, u, btiles[p], brow[p], True)
+        def body(t, carry):
+            p = peer(t)
+            place(local_groups, t, btiles[p], brow[p], True)
             return carry
 
-        lax.fori_loop(0, bound_groups, body, 0)
+        lax.fori_loop(0, n_gy, body, 0)
 
     def place_hub():
-        def body(g, carry):
-            for u in range(GROUP):
-                t = g * GROUP + u
-                place(local_groups + bound_groups + g, u, htiles[t], hcoord[0, t], True)
+        def body(t, carry):
+            place(local_groups + bound_groups, t, htiles[t], hcoord[0, t], True)
             return carry
 
-        lax.fori_loop(0, hub_groups, body, 0)
+        lax.fori_loop(0, hub_groups * GROUP, body, 0)
 
     def local_first(src, self_weight):
         own_part[...] = jnp.dot(
             src[...].reshape(nodes, width), self_weight[...], preferred_element_type=F32
         )
-        acc[...] = local_sum(src, 0)
 
     def local_sum(src, g):
         for u in range(GROUP):
@@ -209,6 +205,8 @@
         return jnp.dot(masked[g], gathered[...], preferred_element_type=F32)
 
     def local_rest(src):
+        acc[...] = local_sum(src, 0)
+
         def body(g, carry):
             acc[...] += local_sum(src, g)
             return carry
@@ -228,6 +226,17 @@
             block_copy(layer, k).wait_recv()
 
     def remote_work(layer):
+        for g in range(bound_groups - 1):
+            wait_blocks(layer, g * GROUP, (g + 1) * GROUP)
+            acc[...] += jnp.dot(
+                masked[local_groups + g],
+                inc[layer, g * GROUP : (g + 1) * GROUP].reshape(GROUP * tile, width),
+                preferred_element_type=F32,
+            )
+        every = slice(0, nodes)
+        wait_blocks(layer, n_gy - 8, n_gy - 2)
+        acc[...] += bound_sum(layer, every, 0, 6)
+
         for k in range(1, n_gx):
             col_copy(layer, k).wait_recv()
         hub_all[...] = hub[layer].astype(F32).reshape(hub_all.shape).astype(BF16)
@@ -244,18 +253,6 @@
 
         lax.fori_loop(0, hub_groups, hub_body, 0)
 
-        for g in range(bound_groups - 1):
-            wait_blocks(layer, g * GROUP, (g + 1) * GROUP)
-            acc[...] += jnp.dot(
-                masked[local_groups + g],
-                inc[layer, g * GROUP : (g + 1) * GROUP].reshape(GROUP * tile, width),
-                preferred_element_type=F32,
-            )
-        every = slice(0, nodes)
-        wait_blocks(layer, n_gy - 8, n_gy - 4)
-        acc[...] += bound_sum(layer, every, 0, 4)
-        wait_blocks(layer, n_gy - 4, n_gy - 2)
-        acc[...] += bound_sum(layer, every, 4, 6)
         wait_blocks(layer, n_gy - 2, n_gy)
 
     def combine(layer, b, neigh_weight):
@@ -280,8 +277,8 @@
     for load in loads[1:]:
         load.wait()
     place_bound()
+    pass_rows_on(0)
     place_hub()
-    pass_rows_on(0)
     place_local()
     local_first(feat, ws1)
     local_rest(feat)

time: 31.7 us -> 31.7 us (level)
  no operation moved by 1% of the time
where the time goes in v4:
time: 31.7 us; the launch traced here: 31.5 us
  Pallas kernels  30.8 us (97%)
  between operations  0.66 us (2%)
    pallas_call x1, Pallas kernels, per_device(): pl.pallas_call(functools.partial(kernel, n_gx, n_gy), out_shape=jax.Shape...  29 us
    pallas_call x1, Pallas kernels, per_device(): pl.pallas_call(store_kernel, out_shape=jax.ShapeDtypeStruct((blocks, tile...  1.83 us

profile of v4, /device:TPU:0, one launch (start us, length us, event | category | flops | bytes accessed | tf_op | source)
XLA Modules:
  0.0 31.5 jit_solution(16821458628086423646)
XLA Ops:
  0.7 29.0 %sage_two_layers.1.src = bf16[8,128,256]{2,1,0:T(8,128)(2,1)} custom-call(s32[8,128]{1,0:T(8,128)} %bitcast.6, s32[2,32]{1,0:T(2,128)} %bitcast.7, s32[1]{0:T(128)S(6)} %copy.16.lcount, s32[8]{0:T(128)} %send.1, s32[8]{0:T(128)} %brow.1, s32[8]{0:T(128)} %hrows.1, s32[2,8]{1,0:T(2,128)} %bitcast.8, bf16[8,128,256]{2,1,0:T(8,128)(2,1)} %bitcast.5, ...), custom_call_target="tpu_custom_call" | custom-call | tf_op jit(solution)/shard_map/sage_two_layers/pallas_call | solution.py:357
  29.6 1.8 %store_result.1 = bf16[8,128,256]{2,1,0:T(8,128)(2,1)} custom-call(bf16[8,128,256]{2,1,0:T(8,128)(2,1)} %sage_two_layers.1.src), custom_call_target="tpu_custom_call" | custom-call | tf_op jit(solution)/shard_map/store_result/pallas_call | solution.py:412
